TPU v7x, 128 devices: a whole 4x4x4 slice. The times are simulated.
128 devices in a mesh: dp: 8 (over x_hi, z), cent: 16 (over x_lo, y, core).
Axes of the slice: x: 4 (x_hi: 2, x_lo: 2; x = x_hi * 2 + x_lo), y: 4, z: 4, core: 2. Of those that a mesh axis runs over, the one named last changes fastest.
Arguments:
- points: bfloat16 [16384, 1024], P(('dp', 'cent')), may hold values from -6 to 6
- centroids: bfloat16 [32768, 1024], P('cent'), may hold values from -6 to 6
Outputs:
- centroids_next: float32 [1024, 32768], P('dp', 'cent')
All inputs are finite; a program needn't handle non-finite values.
Results may differ from a plain program's by a relative error of at most 0.007.
Values may be sent and summed in bfloat16 or wider, within the bound.
No kernel may reach another device: no remote copies, remote signals or barrier semaphores. Data moves between devices by JAX's collectives and lax.ppermute only.
A program may use at most 128 MiB of HBM per device.

v0:
```python
import jax
import jax.numpy as jnp
from jax import lax
from jax.sharding import PartitionSpec as P

BETA_GAIN = 4.0
PRIOR = 0.5


def local(points, centroids):
    features = points.shape[1]
    sharpness = BETA_GAIN * features ** (-0.5)
    gathered = lax.all_gather(points, "cent", axis=0, tiled=True)
    sqnorm = jnp.sum(jnp.square(centroids.astype(jnp.float32)), axis=1)
    total_rows = gathered.shape[0]
    block_rows = min(512, total_rows)
    blocks = gathered.reshape(total_rows // block_rows, block_rows, features)
    shard_cents = centroids.shape[0]

    def logits_of(xblock):
        dots = lax.dot_general(
            xblock, centroids, (((1,), (1,)), ((), ())), preferred_element_type=jnp.float32
        )
        return sharpness * (dots - 0.5 * sqnorm[None, :])

    def resp_of(logits, row_top, row_total):
        return (jnp.exp(logits - row_top[:, None]) / row_total[:, None]).astype(jnp.bfloat16)

    logits = lax.map(logits_of, blocks)
    local_max = jnp.max(logits, axis=-1)
    local_sum = jnp.sum(jnp.exp(logits - local_max[..., None]), axis=-1)
    row_top = lax.pmax(local_max, "cent")
    row_total = lax.psum(local_sum * jnp.exp(local_max - row_top), "cent")
    resp = jax.vmap(resp_of)(logits, row_top, row_total)
    resp = resp.reshape(total_rows, shard_cents)
    counts = jnp.sum(resp.astype(jnp.float32), axis=0)
    dp_count = lax.axis_size("dp")
    dp_index = lax.axis_index("dp")
    column_share = features // dp_count
    numer = lax.psum_scatter(
        lax.dot_general(
            gathered, resp, (((0,), (0,)), ((), ())), preferred_element_type=jnp.float32
        ).astype(jnp.bfloat16),
        "dp",
        scatter_dimension=0,
        tiled=True,
    ).astype(jnp.float32)
    counts_all = lax.psum(counts, "dp")
    own_cols = (
        lax.dynamic_slice_in_dim(centroids, dp_index * column_share, column_share, 1)
        .astype(jnp.float32)
        .T
    )
    result = (numer + PRIOR * own_cols) / (counts_all[None, :] + PRIOR)
    return result


def solution(mesh):
    return jax.shard_map(
        local,
        mesh=mesh,
        in_specs=(P(("dp", "cent"), None), P("cent", None)),
        out_specs=P("dp", "cent"),
        check_vma=False,
    )
```

profile of v0, /device:TPU:0, one launch (start us, length us, event | category | flops | bytes accessed | tf_op | source)
XLA Modules:
  0.0 268.6 jit_solution(6856425457871237441)
XLA Ops:
  6.5 0.0 all-gather.2.cloned.1.call-start
  6.5 0.7 all-gather.2.cloned.1.call-update
  7.3 0.0 reduce-scatter.4.cloned.1.call-start
  7.3 3.1 %multiply_reduce_fusion = f32[2048]{0:T(1024)S(1)} fusion(bf16[2048,1024]{1,0:T(8,128)(2,1)} %param.5), kind=kLoop, calls=%fused_computation.8 | loop fusion | flops 6289408 | bytes 4202496 | tf_op jit(solution)/shard_map/reduce_sum | solution.py:14
  10.4 38.5 %all-gather.2.cloned.1.call-done = bf16[2048,1024]{1,0:T(8,128)(2,1)} async-done(((bf16[128,1024]{1,0:T(8,128)(2,1)}), bf16[2048,1024]{1,0:T(8,128)(2,1)}) %all-gather.2.cloned.1.call-update) | async-done | bytes 4194320 | tf_op jit(solution)/shard_map/all_gather | solution.py:13
  48.9 27.4 %while.10 = (s32[]{:T(128)}, f32[4,512,2048]{2,1,0:T(8,128)}, bf16[4,512,1024]{2,1,0:T(8,128)(2,1)}, bf16[2048,1024]{1,0:T(8,128)(2,1)}, f32[2048]{0:T(1024)S(1)}, /*index=5*/s32[]{:T(128)}) while((s32[]{:T(128)}, f32[4,512,2048]{2,1,0:T(8,128)}, bf16[4,512,1024]{2,1,0:T(8,128)(2,1)}, bf16[2048,1024]{1,0:T(8,128)(2,1)}, f32[2048]{0:T(1024)S(1)}, ...), condition=%wide.region_2.3_spmd, body=%wide.region_1.2_spmd.sunk | while | flops 2149582848 | bytes 9462853 | solution.py:29
  48.9 6.8 %bitcast_dynamic-update-slice_fusion.2 = f32[4,512,2048]{2,1,0:T(8,128)} fusion(f32[4,512,2048]{2,1,0:T(8,128)} %get-tuple-element.83, s32[]{:T(128)} %get-tuple-element.82, bf16[2048,1024]{1,0:T(8,128)(2,1)} %get-tuple-element.91, f32[2048]{0:T(1024)S(1)} %broadcast_multiply_fusion.2, bf16[4,512,1024]{2,1,0:T(8,128)(2,1)} %get-tuple-element.90), kind=kOutput, calls=%fused_computation.clone.1 | convolution fusion | flops 2149580800 | bytes 9446400 | tf_op jit(solution)/shard_map/while/body/eval_jaxpr/dot_general | solution.py:21
  55.7 6.9 %bitcast_dynamic-update-slice_fusion.2 = f32[4,512,2048]{2,1,0:T(8,128)} fusion(f32[4,512,2048]{2,1,0:T(8,128)} %get-tuple-element.83, s32[]{:T(128)} %get-tuple-element.82, bf16[2048,1024]{1,0:T(8,128)(2,1)} %get-tuple-element.91, f32[2048]{0:T(1024)S(1)} %broadcast_multiply_fusion.2, bf16[4,512,1024]{2,1,0:T(8,128)(2,1)} %get-tuple-element.90), kind=kOutput, calls=%fused_computation.clone.1 | convolution fusion | flops 2149580800 | bytes 9446400 | tf_op jit(solution)/shard_map/while/body/eval_jaxpr/dot_general | solution.py:21
  62.6 6.9 %bitcast_dynamic-update-slice_fusion.2 = f32[4,512,2048]{2,1,0:T(8,128)} fusion(f32[4,512,2048]{2,1,0:T(8,128)} %get-tuple-element.83, s32[]{:T(128)} %get-tuple-element.82, bf16[2048,1024]{1,0:T(8,128)(2,1)} %get-tuple-element.91, f32[2048]{0:T(1024)S(1)} %broadcast_multiply_fusion.2, bf16[4,512,1024]{2,1,0:T(8,128)(2,1)} %get-tuple-element.90), kind=kOutput, calls=%fused_computation.clone.1 | convolution fusion | flops 2149580800 | bytes 9446400 | tf_op jit(solution)/shard_map/while/body/eval_jaxpr/dot_general | solution.py:21
  69.4 6.8 %bitcast_dynamic-update-slice_fusion.2 = f32[4,512,2048]{2,1,0:T(8,128)} fusion(f32[4,512,2048]{2,1,0:T(8,128)} %get-tuple-element.83, s32[]{:T(128)} %get-tuple-element.82, bf16[2048,1024]{1,0:T(8,128)(2,1)} %get-tuple-element.91, f32[2048]{0:T(1024)S(1)} %broadcast_multiply_fusion.2, bf16[4,512,1024]{2,1,0:T(8,128)(2,1)} %get-tuple-element.90), kind=kOutput, calls=%fused_computation.clone.1 | convolution fusion | flops 2149580800 | bytes 9446400 | tf_op jit(solution)/shard_map/while/body/eval_jaxpr/dot_general | solution.py:21
  76.3 6.6 %reduce_max.9 = f32[4,512]{1,0:T(4,128)S(1)} reduce(f32[4,512,2048]{2,1,0:T(8,128)} %get-tuple-element.32, f32[]{:T(128)} %constant.20.clone.1), dimensions={2}, to_apply=%region_3.4 | reduce | flops 4192256 | bytes 16785412 | tf_op jit(solution)/shard_map/reduce_max | solution.py:30
  82.9 8.1 %exponential_reduce_fusion = f32[4,512]{1,0:T(4,128)S(1)} fusion(f32[4,512,2048]{2,1,0:T(8,128)} %get-tuple-element.32, f32[4,512]{1,0:T(4,128)S(1)} %reduce_max.9), kind=kLoop, calls=%fused_computation.7 | loop fusion | flops 8386560 | bytes 16793600 | tf_op jit(solution)/shard_map/reduce_sum | solution.py:31
  91.0 29.7 %pmax.7 = f32[4,512]{1,0:T(4,128)S(1)} all-reduce(f32[4,512]{1,0:T(4,128)S(1)} %reduce_max.9), channel_id=1, replica_groups=mesh['dp'=8,'cent'=16] {'cent'}, use_global_device_ids=true, to_apply=%region_4.5 | all-reduce | flops 2048 | bytes 16384 | tf_op jit(solution)/shard_map/pmax | solution.py:32
  120.7 27.8 %psum.14 = f32[4,512]{1,0:T(4,128)S(1)} all-reduce(f32[4,512]{1,0:T(4,128)S(1)} %exponential_multiply_fusion), channel_id=1, replica_groups=mesh['dp'=8,'cent'=16] {'cent'}, use_global_device_ids=true, to_apply=%region_6.7 | all-reduce | flops 2048 | bytes 16384 | tf_op jit(solution)/shard_map/psum | solution.py:33
  148.5 0.0 copy-start
  148.5 8.0 %convert_reduce_fusion = (f32[2048]{0:T(1024)S(1)}, bf16[4,512,2048]{2,1,0:T(8,128)(2,1)S(1)}) fusion(f32[4,512]{1,0:T(4,128)S(1)} %psum.14, f32[4,512,2048]{2,1,0:T(8,128)} %get-tuple-element.32, f32[4,512]{1,0:T(4,128)S(1)} %pmax.7), kind=kLoop, calls=%fused_computation.5 | loop fusion | flops 20969472 | bytes 25190400 | tf_op jit(solution)/shard_map/reduce_sum | solution.py:36
  156.6 0.0 copy-done
  156.6 10.9 %convert_bitcast_fusion = bf16[1024,2048]{0,1:T(8,128)(2,1)} fusion(bf16[2048,2048]{1,0:T(8,128)(2,1)S(1)} %bitcast.23, bf16[2048,1024]{1,0:T(8,128)(2,1)S(1)} %bitcast.25), kind=kOutput, calls=%fused_computation.9 | convolution fusion | flops 8592031744 | bytes 16777216 | tf_op jit(solution)/shard_map/dot_general | solution.py:41
  167.5 6.5 %copy.5 = bf16[1024,2048]{1,0:T(8,128)(2,1)} copy(bf16[1024,2048]{0,1:T(8,128)(2,1)} %convert_bitcast_fusion) | data formatting | bytes 8388608
  174.0 0.0 reduce-scatter.4.cloned.1.call-update
  174.0 24.5 %psum.15 = f32[2048]{0:T(1024)S(1)} all-reduce(f32[2048]{0:T(1024)S(1)} %get-tuple-element.43), channel_id=1, replica_groups=mesh['dp'=8,'cent'=16] {'dp'}, use_global_device_ids=true, to_apply=%region_9.10 | all-reduce | flops 2048 | bytes 16384 | tf_op jit(solution)/shard_map/psum | solution.py:48
  198.6 59.1 %reduce-scatter.4.cloned.1.call-done = bf16[128,2048]{1,0:T(8,128)(2,1)} async-done(((bf16[1024,2048]{1,0:T(8,128)(2,1)}), bf16[128,2048]{1,0:T(8,128)(2,1)}) %reduce-scatter.4.cloned.1.call-update) | async-done | bytes 524304
  257.7 1.3 copy.6
  259.0 1.4 fusion.3
  260.4 1.3 copy.4
  (7 shorter events, 0.0 us)
Async XLA Ops:
  6.5 42.4 %all-gather.2.cloned.1.call-start = ((), (), s32[]{:S(2)}) async-start(), calls=%async_computation.1 | async-start | bytes 4456448 | tf_op jit(solution)/shard_map/all_gather | solution.py:13
  7.3 250.5 %reduce-scatter.4.cloned.1.call-start = ((), (), s32[]{:S(2)}) async-start(), calls=%async_computation.2 | async-start | bytes 4718592
  148.5 8.1 %copy-start = (bf16[4,512,1024]{2,1,0:T(8,128)(2,1)S(1)}, bf16[4,512,1024]{2,1,0:T(8,128)(2,1)}, u32[]{:S(2)}) copy-start(bf16[4,512,1024]{2,1,0:T(8,128)(2,1)} %get-tuple-element.103) | copy-start | bytes 12582916
Sparse Core Ops, SparseCore 0:
  9.1 39.8 all-gather.1
  174.1 83.5 reduce-scatter.3
where the time goes:
time: 269 us
  waiting for transfers between devices  98.4 us (37%)
  blocking collectives  82 us (30%)
  matrix products  38.3 us (14%)
  other arithmetic  27.2 us (10%)
  between operations  13.5 us (5%)
  local copies, waits for them, and re-layouts  9.11 us (3%)
    unnamed x3, waiting for transfers between devices  59.9 us
    all_gather x1, waiting for transfers between devices, local(): gathered = lax.all_gather(points, 'cent', axis=0, tiled=True)  38.5 us
    pmax x1, blocking collectives, local(): row_top = lax.pmax(local_max, 'cent')  29.7 us
    psum x1, blocking collectives, local(): row_total = lax.psum(local_sum * jnp.exp(local_max - row_top), 'cent')  27.8 us
    dot_general x4, matrix products, logits_of(): lax.dot_general(xblock, centroids, (((1,), (1,)), ((), ())), preferred_el...  27.4 us
    psum x1, blocking collectives, local(): counts_all = lax.psum(counts, 'dp')  24.5 us
    dot_general x1, matrix products, local(): lax.dot_general(gathered, resp, (((0,), (0,)), ((), ())), preferred_eleme...  10.9 us
    reduce_sum x1, other arithmetic, local(): local_sum = jnp.sum(jnp.exp(logits - local_max[..., None]), axis=-1)  8.12 us
  transfers between devices with their start and end apart: 2, of which 2 were waited for; matrix products, arithmetic and copies ran while one was open for 1% of the time, Pallas kernels for 0%

commit v1 on v0

--- a/solution.py
+++ b/solution.py
@@ -10,7 +10,9 @@
 def local(points, centroids):
     features = points.shape[1]
     sharpness = BETA_GAIN * features ** (-0.5)
-    gathered = lax.all_gather(points, "cent", axis=0, tiled=True)
+    gathered = jnp.concatenate(
+        lax.all_to_all(jnp.stack([points] * lax.axis_size("cent")), "cent", 0, 0), axis=0
+    )
     sqnorm = jnp.sum(jnp.square(centroids.astype(jnp.float32)), axis=1)
     total_rows = gathered.shape[0]
     block_rows = min(512, total_rows)

time: 269 us -> 302 us (1.12)
  waiting for transfers between devices: 98.4 us -> 112 us
  blocking collectives: 82 us -> 90.5 us
  starting transfers between devices: 0.04 us -> 5.68 us
  local copies, waits for them, and re-layouts: 9.11 us -> 12.6 us
    all_to_all x0 -> x1, waiting for transfers between devices: none -> 53.1 us  [local(): lax.all_to_all(jnp.stack([points] * lax.axis_size('cent')), 'cent', 0, 0)]
    all_gather x1 -> x0, waiting for transfers between devices: 38.5 us -> none  [local(): gathered = lax.all_gather(points, 'cent', axis=0, tiled=True)]
    pmax x1, blocking collectives: 29.7 us -> 37 us  [local(): row_top = lax.pmax(local_max, 'cent')]
    all_to_all x0 -> x1, starting transfers between devices: none -> 5.64 us  [local(): lax.all_to_all(jnp.stack([points] * lax.axis_size('cent')), 'cent', 0, 0)]
    another operation x0 -> x1, local copies, waits for them, and re-layouts: none -> 3.45 us  [local(): jnp.stack([points] * lax.axis_size('cent'))]
    unnamed x3 -> x2, waiting for transfers between devices: 59.9 us -> 58.6 us
    unnamed x4 -> x2, local copies, waits for them, and re-layouts: 7.81 us -> 7.83 us
where the time goes in v1:
time: 302 us; the launch traced here: 301 us
  waiting for transfers between devices  112 us (37%)
  blocking collectives  90.5 us (30%)
  matrix products  39.9 us (13%)
  other arithmetic  27 us (9%)
  between operations  13.5 us (4%)
  local copies, waits for them, and re-layouts  12.6 us (4%)
  starting transfers between devices  5.68 us (2%)
    unnamed x2, waiting for transfers between devices  58.6 us
    all_to_all x1, waiting for transfers between devices, local(): lax.all_to_all(jnp.stack([points] * lax.axis_size('cent')), 'cent', 0, 0)  53.1 us
    pmax x1, blocking collectives, local(): row_top = lax.pmax(local_max, 'cent')  37 us
    psum x1, blocking collectives, local(): row_total = lax.psum(local_sum * jnp.exp(local_max - row_top), 'cent')  27.8 us
    dot_general x4, matrix products, logits_of(): lax.dot_general(xblock, centroids, (((1,), (1,)), ((), ())), preferred_el...  27.4 us
    psum x1, blocking collectives, local(): counts_all = lax.psum(counts, 'dp')  25.7 us
    dot_general x1, matrix products, local(): lax.dot_general(gathered, resp, (((0,), (0,)), ((), ())), preferred_eleme...  12.6 us
    reduce_sum x1, other arithmetic, local(): local_sum = jnp.sum(jnp.exp(logits - local_max[..., None]), axis=-1)  8.12 us
  transfers between devices with their start and end apart: 2, of which 2 were waited for; matrix products, arithmetic and copies ran while one was open for 1% of the time, Pallas kernels for 0%

profile of v1, /device:TPU:0, one launch (start us, length us, event | category | flops | bytes accessed | tf_op | source)
XLA Modules:
  0.0 300.9 jit_solution(12794932032466617155)
XLA Ops:
  6.5 3.5 %stack.2 = bf16[16,128,1024]{2,1,0:T(8,128)(2,1)} broadcast(bf16[128,1024]{1,0:T(8,128)(2,1)} %param.4), dimensions={1,2} | broadcast | bytes 4456448 | tf_op jit(solution)/shard_map/stack | solution.py:14
  10.0 5.6 %all-to-all-start = ((bf16[16,128,1024]{2,1,0:T(8,128)(2,1)}), bf16[16,128,1024]{2,1,0:T(8,128)(2,1)}, u32[]{:S(2)}, u32[]{:S(2)}) async-start(bf16[16,128,1024]{2,1,0:T(8,128)(2,1)} %stack.2), calls=%async_computation | async-start | bytes 8388608 | tf_op jit(solution)/shard_map/all_to_all | solution.py:14
  15.6 0.0 reduce-scatter.4.cloned.1.call-start
  15.7 3.1 %multiply_reduce_fusion = f32[2048]{0:T(1024)S(1)} fusion(bf16[2048,1024]{1,0:T(8,128)(2,1)} %param.5), kind=kLoop, calls=%fused_computation.8 | loop fusion | flops 6289408 | bytes 4202496 | tf_op jit(solution)/shard_map/reduce_sum | solution.py:16
  18.8 53.1 %all-to-all-done = bf16[16,128,1024]{2,1,0:T(8,128)(2,1)} async-done(((bf16[16,128,1024]{2,1,0:T(8,128)(2,1)}), bf16[16,128,1024]{2,1,0:T(8,128)(2,1)}, u32[]{:S(2)}, u32[]{:S(2)}) %all-to-all-start) | async-done | bytes 4194336 | tf_op jit(solution)/shard_map/all_to_all | solution.py:14
  71.9 27.4 %while.10 = (s32[]{:T(128)}, f32[4,512,2048]{2,1,0:T(8,128)}, bf16[4,512,1024]{2,1,0:T(8,128)(2,1)}, bf16[2048,1024]{1,0:T(8,128)(2,1)}, f32[2048]{0:T(1024)S(1)}, /*index=5*/s32[]{:T(128)}) while((s32[]{:T(128)}, f32[4,512,2048]{2,1,0:T(8,128)}, bf16[4,512,1024]{2,1,0:T(8,128)(2,1)}, bf16[2048,1024]{1,0:T(8,128)(2,1)}, f32[2048]{0:T(1024)S(1)}, ...), condition=%wide.region_2.3_spmd, body=%wide.region_1.2_spmd.sunk | while | flops 2149582848 | bytes 9462853 | solution.py:31
  71.9 6.8 %bitcast_dynamic-update-slice_fusion.2 = f32[4,512,2048]{2,1,0:T(8,128)} fusion(f32[4,512,2048]{2,1,0:T(8,128)} %get-tuple-element.83, s32[]{:T(128)} %get-tuple-element.82, bf16[2048,1024]{1,0:T(8,128)(2,1)} %get-tuple-element.91, f32[2048]{0:T(1024)S(1)} %broadcast_multiply_fusion.2, bf16[4,512,1024]{2,1,0:T(8,128)(2,1)} %get-tuple-element.90), kind=kOutput, calls=%fused_computation.clone.1 | convolution fusion | flops 2149580800 | bytes 9446400 | tf_op jit(solution)/shard_map/while/body/eval_jaxpr/dot_general | solution.py:23
  78.7 6.9 %bitcast_dynamic-update-slice_fusion.2 = f32[4,512,2048]{2,1,0:T(8,128)} fusion(f32[4,512,2048]{2,1,0:T(8,128)} %get-tuple-element.83, s32[]{:T(128)} %get-tuple-element.82, bf16[2048,1024]{1,0:T(8,128)(2,1)} %get-tuple-element.91, f32[2048]{0:T(1024)S(1)} %broadcast_multiply_fusion.2, bf16[4,512,1024]{2,1,0:T(8,128)(2,1)} %get-tuple-element.90), kind=kOutput, calls=%fused_computation.clone.1 | convolution fusion | flops 2149580800 | bytes 9446400 | tf_op jit(solution)/shard_map/while/body/eval_jaxpr/dot_general | solution.py:23
  85.5 6.9 %bitcast_dynamic-update-slice_fusion.2 = f32[4,512,2048]{2,1,0:T(8,128)} fusion(f32[4,512,2048]{2,1,0:T(8,128)} %get-tuple-element.83, s32[]{:T(128)} %get-tuple-element.82, bf16[2048,1024]{1,0:T(8,128)(2,1)} %get-tuple-element.91, f32[2048]{0:T(1024)S(1)} %broadcast_multiply_fusion.2, bf16[4,512,1024]{2,1,0:T(8,128)(2,1)} %get-tuple-element.90), kind=kOutput, calls=%fused_computation.clone.1 | convolution fusion | flops 2149580800 | bytes 9446400 | tf_op jit(solution)/shard_map/while/body/eval_jaxpr/dot_general | solution.py:23
  92.4 6.8 %bitcast_dynamic-update-slice_fusion.2 = f32[4,512,2048]{2,1,0:T(8,128)} fusion(f32[4,512,2048]{2,1,0:T(8,128)} %get-tuple-element.83, s32[]{:T(128)} %get-tuple-element.82, bf16[2048,1024]{1,0:T(8,128)(2,1)} %get-tuple-element.91, f32[2048]{0:T(1024)S(1)} %broadcast_multiply_fusion.2, bf16[4,512,1024]{2,1,0:T(8,128)(2,1)} %get-tuple-element.90), kind=kOutput, calls=%fused_computation.clone.1 | convolution fusion | flops 2149580800 | bytes 9446400 | tf_op jit(solution)/shard_map/while/body/eval_jaxpr/dot_general | solution.py:23
  99.2 6.6 %reduce_max.9 = f32[4,512]{1,0:T(4,128)S(1)} reduce(f32[4,512,2048]{2,1,0:T(8,128)} %get-tuple-element.32, f32[]{:T(128)} %constant.20.clone.1), dimensions={2}, to_apply=%region_3.4 | reduce | flops 4192256 | bytes 16785412 | tf_op jit(solution)/shard_map/reduce_max | solution.py:32
  105.8 8.1 %exponential_reduce_fusion = f32[4,512]{1,0:T(4,128)S(1)} fusion(f32[4,512,2048]{2,1,0:T(8,128)} %get-tuple-element.32, f32[4,512]{1,0:T(4,128)S(1)} %reduce_max.9), kind=kLoop, calls=%fused_computation.7 | loop fusion | flops 8386560 | bytes 16793600 | tf_op jit(solution)/shard_map/reduce_sum | solution.py:33
  113.9 37.0 %pmax.7 = f32[4,512]{1,0:T(4,128)S(1)} all-reduce(f32[4,512]{1,0:T(4,128)S(1)} %reduce_max.9), channel_id=1, replica_groups=mesh['dp'=8,'cent'=16] {'cent'}, use_global_device_ids=true, to_apply=%region_4.5 | all-reduce | flops 2048 | bytes 16384 | tf_op jit(solution)/shard_map/pmax | solution.py:34
  150.9 27.8 %psum.14 = f32[4,512]{1,0:T(4,128)S(1)} all-reduce(f32[4,512]{1,0:T(4,128)S(1)} %exponential_multiply_fusion), channel_id=1, replica_groups=mesh['dp'=8,'cent'=16] {'cent'}, use_global_device_ids=true, to_apply=%region_6.7 | all-reduce | flops 2048 | bytes 16384 | tf_op jit(solution)/shard_map/psum | solution.py:35
  178.8 7.8 %convert_reduce_fusion = (f32[2048]{0:T(1024)S(1)}, bf16[4,512,2048]{2,1,0:T(8,128)(2,1)S(1)}) fusion(f32[4,512]{1,0:T(4,128)S(1)} %psum.14, f32[4,512,2048]{2,1,0:T(8,128)} %get-tuple-element.32, f32[4,512]{1,0:T(4,128)S(1)} %pmax.7), kind=kLoop, calls=%fused_computation.5 | loop fusion | flops 20969472 | bytes 25190400 | tf_op jit(solution)/shard_map/reduce_sum | solution.py:38
  186.6 12.6 %convert_bitcast_fusion = bf16[1024,2048]{0,1:T(8,128)(2,1)} fusion(bf16[2048,2048]{1,0:T(8,128)(2,1)S(1)} %bitcast.24, bf16[2048,1024]{1,0:T(8,128)(2,1)} %bitcast.4), kind=kOutput, calls=%fused_computation.9 | convolution fusion | flops 8592031744 | bytes 16777216 | tf_op jit(solution)/shard_map/dot_general | solution.py:43
  199.1 6.5 %copy.5 = bf16[1024,2048]{1,0:T(8,128)(2,1)} copy(bf16[1024,2048]{0,1:T(8,128)(2,1)} %convert_bitcast_fusion) | data formatting | bytes 8388608
  205.7 0.0 reduce-scatter.4.cloned.1.call-update
  205.7 25.7 %psum.15 = f32[2048]{0:T(1024)S(1)} all-reduce(f32[2048]{0:T(1024)S(1)} %get-tuple-element.43), channel_id=1, replica_groups=mesh['dp'=8,'cent'=16] {'dp'}, use_global_device_ids=true, to_apply=%region_9.10 | all-reduce | flops 2048 | bytes 16384 | tf_op jit(solution)/shard_map/psum | solution.py:50
  231.4 58.6 %reduce-scatter.4.cloned.1.call-done = bf16[128,2048]{1,0:T(8,128)(2,1)} async-done(((bf16[1024,2048]{1,0:T(8,128)(2,1)}), bf16[128,2048]{1,0:T(8,128)(2,1)}) %reduce-scatter.4.cloned.1.call-update) | async-done | bytes 524304
  290.0 1.3 copy.6
  291.3 1.4 fusion.3
  292.7 1.3 copy.4
  (7 shorter events, 0.0 us)
Async XLA Ops:
  10.0 61.9 %all-to-all-start = ((bf16[16,128,1024]{2,1,0:T(8,128)(2,1)}), bf16[16,128,1024]{2,1,0:T(8,128)(2,1)}, u32[]{:S(2)}, u32[]{:S(2)}) async-start(bf16[16,128,1024]{2,1,0:T(8,128)(2,1)} %stack.2), calls=%async_computation | async-start | bytes 8388608 | tf_op jit(solution)/shard_map/all_to_all | solution.py:14
  15.6 274.4 %reduce-scatter.4.cloned.1.call-start = ((), (), s32[]{:S(2)}) async-start(), calls=%async_computation.2 | async-start | bytes 4718592
Sparse Core Ops, SparseCore 0:
  205.8 84.1 reduce-scatter.3
